TPU v7x, 256 devices: a whole 4x4x8 slice. The times are simulated.
256 devices in a mesh: section: 4 (over z_lo), dp: 64 (over x, y, z_hi, core).
Axes of the slice: x: 4, y: 4, z: 8 (z_hi: 2, z_lo: 4; z = z_hi * 4 + z_lo), core: 2. Of those that a mesh axis runs over, the one named last changes fastest.
Arguments:
- section_inputs: bfloat16 [4, 12544, 2048], P('section', 'dp'), may hold values from -16 to 16
- norm_gain: float32 [4, 2048], P('section'), may hold values from 0.25 to 1.75
- query_gain: float32 [4, 2048], P('section'), may hold values from -5 to 5
- key_gain: float32 [4, 2048], P('section'), may hold values from -5 to 5
- output_weight: bfloat16 [4, 2048, 2048], P('section', 'dp'), may hold values from -0.125 to 0.125
- full_sequence_gradient: bfloat16 [256, 196, 2048], P('dp'), may hold values from -6 to 6
- patch_order: int32 [256, 196], P('dp'), may hold values from 0 to 195, each once within a row
Outputs:
- input_grads: bfloat16 [4, 12544, 2048], P('section', 'dp')
- weight_grads: float32 [4, 2048, 2048], P('section', 'dp')
- gain_grads: float32 [4, 3, 2048], P('section')
Inputs may be any that keep to these rules, and one draw needn't show every extreme that they name: `patch_order`: each row holds every patch number once; the first 49 are the kept patches.
All inputs are finite; a program needn't handle non-finite values.
Results may differ from a plain program's by a relative error of at most 0.0057.
Values may be sent and summed in bfloat16 or wider, within the bound.
A program may use at most 128 MiB of HBM per device.

v0:
```python
import math
import jax
import jax.numpy as jnp
from jax import lax
from jax.sharding import PartitionSpec as P

HEADS = 16
KEPT = 49
PATCHES = 196
MICRO = 2
highest = lax.Precision.HIGHEST


def from_behind(block, axis, distance):
    devices = range(lax.axis_size(axis))
    route = [(i - distance, i) for i in devices if i - distance in devices]
    return lax.ppermute(block, axis, route)


def normalize(inputs):
    values = inputs.astype(jnp.float32)
    centred = values - jnp.mean(values, axis=-1, keepdims=True)
    variance = jnp.mean(centred * centred, axis=-1, keepdims=True)
    inverse = lax.rsqrt(variance + 1e-06)
    return (centred * inverse, inverse)


def attend_forward(normed, gain_row, query_row, key_row, heads):
    row_count, feature_width = normed.shape
    head_width = feature_width // heads
    split_shape = (row_count // KEPT, KEPT, heads, head_width)
    hidden = normed * gain_row
    queries = (hidden * query_row).reshape(split_shape)
    key_rows = (hidden * key_row).reshape(split_shape)
    value_rows = hidden.reshape(split_shape)
    attention_logits = jnp.einsum(
        "bqhd,bkhd->bhqk", queries, key_rows, precision=highest
    ) / math.sqrt(head_width)
    softmaxed = jax.nn.softmax(attention_logits, axis=-1)
    mixed = jnp.einsum("bhqk,bkhd->bqhd", softmaxed, value_rows, precision=highest)
    return (
        hidden,
        queries,
        key_rows,
        value_rows,
        softmaxed,
        mixed.reshape(row_count, feature_width).astype(jnp.bfloat16),
    )


def attend_backward(
    cotangent,
    back,
    normed,
    inverse,
    hidden,
    queries,
    key_rows,
    value_rows,
    softmaxed,
    gain_row,
    query_row,
    key_row,
):
    row_count, feature_width = back.shape
    head_width = queries.shape[-1]
    back_split = back.reshape(queries.shape)
    soft_grad = jnp.einsum("bqhd,bkhd->bhqk", back_split, value_rows, precision=highest)
    value_grad = jnp.einsum("bhqk,bqhd->bkhd", softmaxed, back_split, precision=highest).reshape(
        row_count, feature_width
    )
    score_grad = (
        softmaxed
        * (soft_grad - jnp.sum(soft_grad * softmaxed, axis=-1, keepdims=True))
        / math.sqrt(head_width)
    )
    query_grad = jnp.einsum("bhqk,bkhd->bqhd", score_grad, key_rows, precision=highest).reshape(
        row_count, feature_width
    )
    key_grad = jnp.einsum("bhqk,bqhd->bkhd", score_grad, queries, precision=highest).reshape(
        row_count, feature_width
    )
    hidden_grad = query_grad * query_row + key_grad * key_row + value_grad
    normed_grad = hidden_grad * gain_row
    first_mean = jnp.mean(normed_grad, axis=-1, keepdims=True)
    second_mean = jnp.mean(normed_grad * normed, axis=-1, keepdims=True)
    input_grad = (
        cotangent.astype(jnp.float32) + inverse * (normed_grad - first_mean - normed * second_mean)
    ).astype(jnp.bfloat16)
    sums = jnp.stack(
        [
            jnp.sum(hidden_grad * normed, axis=0),
            jnp.sum(query_grad * hidden, axis=0),
            jnp.sum(key_grad * hidden, axis=0),
        ]
    )
    return (input_grad, sums)


def shards(
    section_inputs,
    norm_gain,
    query_gain,
    key_gain,
    output_weight,
    full_sequence_gradient,
    patch_order,
):
    inputs = section_inputs[0]
    row_count, feature_width = inputs.shape
    image_count = row_count // KEPT
    section = lax.axis_index("section")
    sections = lax.axis_size("section")
    all_images = image_count * lax.axis_size("dp")
    gain_row = norm_gain[0]
    query_row = query_gain[0]
    key_row = key_gain[0]
    weight = lax.all_gather(output_weight[0], "dp", axis=0, tiled=True)
    normed, inverse = normalize(inputs)
    hidden, queries, key_rows, value_rows, softmaxed, mixed = attend_forward(
        normed, gain_row, query_row, key_row, HEADS
    )
    kept = patch_order[:, :KEPT]
    chosen_patches = (
        kept[:, :, None] == jnp.arange(PATCHES, dtype=jnp.int32)[None, None, :]
    ).astype(jnp.bfloat16)
    upper_bound = (
        jnp.einsum(
            "usn,unj->usj",
            chosen_patches,
            full_sequence_gradient,
            preferred_element_type=jnp.float32,
        )
        .astype(jnp.bfloat16)
        .reshape(row_count, feature_width)
    )
    per_unit = image_count // MICRO
    unit_rows = per_unit * KEPT
    unit_count = image_count // per_unit
    step_count = unit_count + sections - 1

    def take_rows(array, unit):
        return lax.dynamic_slice_in_dim(array, unit * unit_rows, unit_rows, 0)

    def take_images(array, unit):
        return lax.dynamic_slice_in_dim(array, unit * per_unit, per_unit, 0)

    def put_rows(array, piece, unit, valid):
        present_value = take_rows(array, unit)
        return lax.dynamic_update_slice_in_dim(
            array, jnp.where(valid, piece, present_value), unit * unit_rows, 0
        )

    def advance(step_index, carry):
        received, cotangents, input_grads, sums, running_weight = carry
        unit = step_index - (sections - 1 - section)
        valid = jnp.logical_and(unit >= 0, unit < unit_count)
        safe_unit = jnp.clip(unit, 0, unit_count - 1)
        cotangent = jnp.where(section == sections - 1, take_rows(upper_bound, safe_unit), received)
        back = lax.dot_general(
            cotangent, weight, (((1,), (1,)), ((), ())), preferred_element_type=jnp.float32
        )
        input_grad, partial_sums = attend_backward(
            cotangent,
            back,
            take_rows(normed, safe_unit),
            take_rows(inverse, safe_unit),
            take_rows(hidden, safe_unit),
            take_images(queries, safe_unit),
            take_images(key_rows, safe_unit),
            take_images(value_rows, safe_unit),
            take_images(softmaxed, safe_unit),
            gain_row,
            query_row,
            key_row,
        )
        cotangents = put_rows(cotangents, cotangent, safe_unit, valid)
        input_grads = put_rows(input_grads, input_grad, safe_unit, valid)
        sums = sums + jnp.where(valid, partial_sums, 0.0)
        received = from_behind(input_grad, "section", -1)
        return (received, cotangents, input_grads, sums, running_weight)

    weight_offset = jnp.zeros((1,), jnp.float32)
    start_carry = (
        jnp.zeros((unit_rows, feature_width), jnp.bfloat16),
        jnp.zeros_like(inputs),
        jnp.zeros_like(inputs),
        jnp.zeros((3, feature_width), jnp.float32),
        weight_offset,
    )
    final_carry = lax.fori_loop(0, step_count, advance, start_carry)
    cotangents = final_carry[1]
    input_grads = final_carry[2]
    gain_total = lax.psum(final_carry[3], "dp") / all_images
    weight_share = (
        lax.psum_scatter(
            lax.dot_general(
                mixed, cotangents, (((0,), (0,)), ((), ())), preferred_element_type=jnp.float32
            ),
            "dp",
            scatter_dimension=0,
            tiled=True,
        )
        / all_images
    )
    return (input_grads[None], weight_share[None], gain_total[None])


def solution(mesh):
    return jax.shard_map(
        shards,
        mesh=mesh,
        in_specs=(
            P("section", "dp", None),
            P("section", None),
            P("section", None),
            P("section", None),
            P("section", "dp", None),
            P("dp", None, None),
            P("dp", None),
        ),
        out_specs=(P("section", "dp", None), P("section", "dp", None), P("section", None, None)),
        check_vma=False,
    )
```

profile of v0, /device:TPU:96, one launch (start us, length us, event | category | flops | bytes accessed | tf_op | source)
XLA Modules:
  0.0 857.8 jit_solution(7415387619002725321)
XLA Ops:
  12.7 4.7 fusion.17
  26.9 4.0 multiply_reduce_fusion.6
  32.1 3.7 fusion.23
  39.3 82.6 %all-gather.3.cloned.1.call-done = bf16[1,2048,2048]{2,1,0:T(8,128)(2,1)} async-done(((bf16[1,32,2048]{2,1,0:T(8,128)(2,1)}), bf16[1,2048,2048]{2,1,0:T(8,128)(2,1)}) %all-gather.3.cloned.1.call-update) | async-done | bytes 8388624 | tf_op jit(solution)/shard_map/all_gather | solution.py:118
  124.6 193.8 %while.22 = (s32[]{:T(128)}, bf16[98,2048]{1,0:T(8,128)(2,1)}, bf16[196,2048]{1,0:T(8,128)(2,1)}, bf16[196,2048]{1,0:T(8,128)(2,1)}, f32[3,2048]{1,0:T(4,128)S(1...) while((s32[]{:T(128)}, bf16[98,2048]{1,0:T(8,128)(2,1)}, ...), condition=%wide.region_11.12_spmd.clone, body=%wide.region_4.11_spmd.clone.sunk | while | flops 1300798208 | bytes 88767504 | solution.py:191
  126.9 6.1 fusion.47
  150.6 5.7 collective-permute-start
  156.2 3.3 dynamic_update_slice.22
  159.5 3.3 dynamic_update_slice.23
  167.5 6.1 fusion.47
  191.1 5.3 collective-permute-start
  199.6 3.1 dynamic_update_slice.23
  206.9 6.1 fusion.47
  230.5 5.3 collective-permute-start
  238.9 3.1 dynamic_update_slice.23
  245.3 6.1 fusion.47
  269.0 5.3 collective-permute-start
  277.4 3.1 dynamic_update_slice.23
  283.0 6.1 fusion.47
  306.6 5.3 collective-permute-start
  315.0 3.1 dynamic_update_slice.23
  318.4 9.5 %fusion.30 = f32[2048,2048]{1,0:T(8,128)} fusion(bf16[196,2048]{1,0:T(8,128)(2,1)} %bitcast.137, bf16[196,2048]{1,0:T(8,128)(2,1)} %get-tuple-element.412), kind=kOutput, calls=%fused_computation.62 | convolution fusion | flops 1644167168 | bytes 18382848 | tf_op jit(solution)/shard_map/dot_general | solution.py:197
  328.0 425.0 %psum.7 = f32[3,2048]{1,0:T(4,128)S(1)} all-reduce(f32[3,2048]{1,0:T(4,128)S(1)} %get-tuple-element.413), channel_id=1, replica_groups=mesh['section'=4,'dp'=64] {'dp'}, use_global_device_ids=true, to_apply=%region_13.14 | all-reduce | flops 6144 | bytes 49152 | tf_op jit(solution)/shard_map/psum | solution.py:194
  753.7 95.6 %reduce-scatter.2.cloned.1.call-done = f32[32,2048]{1,0:T(8,128)} async-done(((f32[2048,2048]{1,0:T(8,128)}), f32[32,2048]{1,0:T(8,128)}) %reduce-scatter.2.cloned.1.call-update) | async-done | bytes 262160 | tf_op jit(solution)/shard_map/reduce_scatter | solution.py:196
  (244 shorter events, 140.9 us)
Async XLA Ops:
  7.2 5.5 copy-start
  7.2 114.7 %all-gather.3.cloned.1.call-start = ((), (), s32[]{:S(2)}) async-start(), calls=%async_computation.2 | async-start | bytes 8519680 | tf_op jit(solution)/shard_map/all_gather | solution.py:118
  7.9 841.4 %reduce-scatter.2.cloned.1.call-start = ((), (), s32[]{:S(2)}) async-start(), calls=%async_computation.1 | async-start | bytes 17039360 | tf_op jit(solution)/shard_map/reduce_scatter | solution.py:196
  8.0 2.8 copy-start.8
  8.0 4.7 slice-start
  17.4 2.5 copy-start.11
  133.2 3.1 copy-start.6
  148.7 7.5 copy-start.4
  150.6 14.7 %collective-permute-start = (bf16[98,2048]{1,0:T(8,128)(2,1)}, bf16[98,2048]{1,0:T(8,128)(2,1)}, u32[]{:S(2)}, u32[]{:S(2)}) collective-permute-start(bf16[98,2048]{1,0:T(8,128)(2,1)} %get-tuple-element.688), channel_id=1, source_target_pairs={{64,0},{128,64},{192,128},{65,1},{129,65},{193,129},{66,2},{130,66... | collective-permute-start | bytes 1204232 | tf_op jit(solution)/shard_map/while/body/eval_jaxpr/ppermute | solution.py:17
  173.8 3.1 copy-start.6
  186.7 1.9 copy-start.7
  189.3 7.2 copy-start.4
  191.1 13.4 %collective-permute-start = (bf16[98,2048]{1,0:T(8,128)(2,1)}, bf16[98,2048]{1,0:T(8,128)(2,1)}, u32[]{:S(2)}, u32[]{:S(2)}) collective-permute-start(bf16[98,2048]{1,0:T(8,128)(2,1)} %get-tuple-element.688), channel_id=1, source_target_pairs={{64,0},{128,64},{192,128},{65,1},{129,65},{193,129},{66,2},{130,66... | collective-permute-start | bytes 1204232 | tf_op jit(solution)/shard_map/while/body/eval_jaxpr/ppermute | solution.py:17
  213.2 3.1 copy-start.6
  226.1 1.9 copy-start.7
  228.6 7.2 copy-start.4
  230.5 12.6 %collective-permute-start = (bf16[98,2048]{1,0:T(8,128)(2,1)}, bf16[98,2048]{1,0:T(8,128)(2,1)}, u32[]{:S(2)}, u32[]{:S(2)}) collective-permute-start(bf16[98,2048]{1,0:T(8,128)(2,1)} %get-tuple-element.688), channel_id=1, source_target_pairs={{64,0},{128,64},{192,128},{65,1},{129,65},{193,129},{66,2},{130,66... | collective-permute-start | bytes 1204232 | tf_op jit(solution)/shard_map/while/body/eval_jaxpr/ppermute | solution.py:17
  251.7 3.1 copy-start.6
  267.1 7.2 copy-start.4
  269.0 11.7 %collective-permute-start = (bf16[98,2048]{1,0:T(8,128)(2,1)}, bf16[98,2048]{1,0:T(8,128)(2,1)}, u32[]{:S(2)}, u32[]{:S(2)}) collective-permute-start(bf16[98,2048]{1,0:T(8,128)(2,1)} %get-tuple-element.688), channel_id=1, source_target_pairs={{64,0},{128,64},{192,128},{65,1},{129,65},{193,129},{66,2},{130,66... | collective-permute-start | bytes 1204232 | tf_op jit(solution)/shard_map/while/body/eval_jaxpr/ppermute | solution.py:17
  289.3 3.1 copy-start.6
  304.7 7.2 copy-start.4
  306.6 11.6 %collective-permute-start = (bf16[98,2048]{1,0:T(8,128)(2,1)}, bf16[98,2048]{1,0:T(8,128)(2,1)}, u32[]{:S(2)}, u32[]{:S(2)}) collective-permute-start(bf16[98,2048]{1,0:T(8,128)(2,1)} %get-tuple-element.688), channel_id=1, source_target_pairs={{64,0},{128,64},{192,128},{65,1},{129,65},{193,129},{66,2},{130,66... | collective-permute-start | bytes 1204232 | tf_op jit(solution)/shard_map/while/body/eval_jaxpr/ppermute | solution.py:17
  328.0 523.0 %copy-start.1 = (bf16[4,196,2048]{2,0,1:T(4,128)(2,1)S(1)}, bf16[4,196,2048]{2,0,1:T(4,128)(2,1)}, u32[]{:S(2)}) copy-start(bf16[4,196,2048]{2,0,1:T(4,128)(2,1)} %param.14) | copy-start | bytes 9633796
  (27 other events, 39.5 us)
Sparse Core Ops, SparseCore 0:
  11.5 110.3 all-gather.2
  328.1 521.1 reduce-scatter.1
where the time goes:
time: 860 us; the launch traced here: 858 us
  blocking collectives  425 us (49%)
  waiting for transfers between devices  184 us (21%)
  matrix products  95.3 us (11%)
  local copies, waits for them, and re-layouts  80 us (9%)
  other arithmetic  31.3 us (4%)
  starting transfers between devices  26.8 us (3%)
  between operations  14.2 us (2%)
    psum x1, blocking collectives, shards(): gain_total = lax.psum(final_carry[3], 'dp') / all_images  425 us
    reduce_scatter x1, waiting for transfers between devices, shards(): lax.psum_scatter(lax.dot_general(mixed, cotangents, (((0,), (0,)), ((), (...  95.6 us
    all_gather x1, waiting for transfers between devices, shards(): weight = lax.all_gather(output_weight[0], 'dp', axis=0, tiled=True)  82.6 us
    dynamic_update_slice x10, local copies, waits for them, and re-layouts, put_rows(): lax.dynamic_update_slice_in_dim(array, jnp.where(valid, piece, present_va...  31.8 us
    dot_general x5, matrix products, advance(): lax.dot_general(cotangent, weight, (((1,), (1,)), ((), ())), preferred_el...  30.5 us
    ppermute x5, starting transfers between devices, from_behind(): return lax.ppermute(block, axis, route)  26.7 us
    while x110, local copies, waits for them, and re-layouts  22.4 us
    select_n x10, other arithmetic, put_rows(): jnp.where(valid, piece, present_value)  17.9 us
  transfers between devices with their start and end apart: 7, of which 6 were waited for; matrix products, arithmetic and copies ran while one was open for 7% of the time, Pallas kernels for 0%

commit v1 on v0

--- a/solution.py
+++ b/solution.py
@@ -9,6 +9,14 @@
 PATCHES = 196
 MICRO = 2
 highest = lax.Precision.HIGHEST
+
+
+def put_marks(tile_in):
+    spare = lax.axis_size("dp")
+    arr_now = lax.all_to_all(
+        jnp.stack(spare * [tile_in], axis=0), axis_name="dp", split_axis=0, concat_axis=0
+    )
+    return jnp.concatenate(arr_now, axis=0)
 
 
 def from_behind(block, axis, distance):
@@ -115,7 +123,7 @@
     gain_row = norm_gain[0]
     query_row = query_gain[0]
     key_row = key_gain[0]
-    weight = lax.all_gather(output_weight[0], "dp", axis=0, tiled=True)
+    weight = put_marks(output_weight[0])
     normed, inverse = normalize(inputs)
     hidden, queries, key_rows, value_rows, softmaxed, mixed = attend_forward(
         normed, gain_row, query_row, key_row, HEADS

time: 860 us -> 952 us (1.11)
  waiting for transfers between devices: 184 us -> 267 us
    all_to_all x0 -> x1, waiting for transfers between devices: none -> 159 us  [put_marks(): lax.all_to_all(jnp.stack(spare * [tile_in], axis=0), axis_name='dp', spli...]
    all_gather x1 -> x0, waiting for transfers between devices: 82.6 us -> none  [shards(): weight = lax.all_gather(output_weight[0], 'dp', axis=0, tiled=True)]
    all_to_all x0 -> x1, starting transfers between devices: none -> 12.1 us  [put_marks(): lax.all_to_all(jnp.stack(spare * [tile_in], axis=0), axis_name='dp', spli...]
    while x110 -> x80, local copies, waits for them, and re-layouts: 22.4 us -> 13.8 us
  transfers between devices with their start and end apart: 7 -> 7, of which waited for: 6 -> 5; matrix products, arithmetic and copies ran while one was open for 7% -> 7% of each run, Pallas kernels for 0% -> 0%
where the time goes in v1:
time: 952 us; the launch traced here: 946 us
  blocking collectives  427 us (45%)
  waiting for transfers between devices  267 us (28%)
  matrix products  96.6 us (10%)
  local copies, waits for them, and re-layouts  71.4 us (8%)
  other arithmetic  38.4 us (4%)
  starting transfers between devices  30.5 us (3%)
  between operations  14.2 us (1%)
    psum x1, blocking collectives, shards(): gain_total = lax.psum(final_carry[3], 'dp') / all_images  427 us
    all_to_all x1, waiting for transfers between devices, put_marks(): lax.all_to_all(jnp.stack(spare * [tile_in], axis=0), axis_name='dp', spli...  159 us
    reduce_scatter x1, waiting for transfers between devices, shards(): lax.psum_scatter(lax.dot_general(mixed, cotangents, (((0,), (0,)), ((), (...  103 us
    dynamic_update_slice x10, local copies, waits for them, and re-layouts, put_rows(): lax.dynamic_update_slice_in_dim(array, jnp.where(valid, piece, present_va...  33.5 us
    dot_general x5, matrix products, advance(): lax.dot_general(cotangent, weight, (((1,), (1,)), ((), ())), preferred_el...  30.5 us
    select_n x10, other arithmetic, put_rows(): jnp.where(valid, piece, present_value)  25 us
  transfers between devices with their start and end apart: 7, of which 5 were waited for; matrix products, arithmetic and copies ran while one was open for 7% of the time, Pallas kernels for 0%

profile of v1, /device:TPU:96, one launch (start us, length us, event | category | flops | bytes accessed | tf_op | source)
XLA Modules:
  0.0 946.3 jit_solution(16603692737164646509)
XLA Ops:
  7.2 5.3 stack.39
  12.5 12.1 %all-to-all-start = ((bf16[64,32,2048]{2,1,0:T(8,128)(2,1)}), bf16[64,32,2048]{2,1,0:T(8,128)(2,1)}, u32[]{:S(2)}, u32[]{:S(2)}) async-start(bf16[64,32,2048]{2,1,0:T(8,128)(2,1)} %stack.39), calls=%async_computation | async-start | bytes 16777216 | tf_op jit(solution)/shard_map/all_to_all | solution.py:16
  38.1 4.7 fusion.17
  45.2 5.4 multiply_reduce_fusion.6
  52.5 3.7 fusion.23
  59.9 158.9 %all-to-all-done = bf16[64,32,2048]{2,1,0:T(8,128)(2,1)} async-done(((bf16[64,32,2048]{2,1,0:T(8,128)(2,1)}), bf16[64,32,2048]{2,1,0:T(8,128)(2,1)}, u32[]{:S(2)}, u32[]{:S(2)}) %all-to-all-start) | async-done | bytes 8388640 | tf_op jit(solution)/shard_map/all_to_all | solution.py:16
  220.8 176.3 %while.22 = (s32[]{:T(128)}, bf16[98,2048]{1,0:T(8,128)(2,1)S(1)}, bf16[196,2048]{1,0:T(8,128)(2,1)}, bf16[196,2048]{1,0:T(8,128)(2,1)}, f32[3,2048]{1,0:T(4,128...) while((s32[]{:T(128)}, bf16[98,2048]{1,0:T(8,128)(2,1)S(1)}, ...), condition=%wide.region_11.12_spmd.clone, body=%wide.region_4.11_spmd.clone.sunk | while | flops 1300798208 | bytes 80739248 | solution.py:199
  223.1 6.1 fusion.47
  246.1 3.4 dynamic_update_slice.23
  249.5 3.4 dynamic_update_slice.22
  257.4 6.1 fusion.47
  279.0 4.3 collective-permute-start
  283.4 3.3 dynamic_update_slice.23
  293.9 6.1 fusion.47
  315.5 4.3 collective-permute-start
  319.8 3.3 dynamic_update_slice.23
  329.5 6.1 fusion.47
  351.1 4.3 collective-permute-start
  355.4 3.3 dynamic_update_slice.23
  364.4 6.1 fusion.47
  386.0 4.1 collective-permute-start
  397.1 9.5 %fusion.30 = f32[2048,2048]{1,0:T(8,128)} fusion(bf16[196,2048]{1,0:T(8,128)(2,1)} %bitcast.137, bf16[196,2048]{1,0:T(8,128)(2,1)} %get-tuple-element.412), kind=kOutput, calls=%fused_computation.62 | convolution fusion | flops 1644167168 | bytes 18382848 | tf_op jit(solution)/shard_map/dot_general | solution.py:205
  406.6 427.5 %psum.7 = f32[3,2048]{1,0:T(4,128)S(1)} all-reduce(f32[3,2048]{1,0:T(4,128)S(1)} %get-tuple-element.413), channel_id=1, replica_groups=mesh['section'=4,'dp'=64] {'dp'}, use_global_device_ids=true, to_apply=%region_13.14 | all-reduce | flops 6144 | bytes 49152 | tf_op jit(solution)/shard_map/psum | solution.py:202
  834.8 103.1 %reduce-scatter.2.cloned.1.call-done = f32[32,2048]{1,0:T(8,128)} async-done(((f32[2048,2048]{1,0:T(8,128)}), f32[32,2048]{1,0:T(8,128)}) %reduce-scatter.2.cloned.1.call-update) | async-done | bytes 262160 | tf_op jit(solution)/shard_map/reduce_scatter | solution.py:204
  (222 shorter events, 136.3 us)
Async XLA Ops:
  7.2 30.9 %copy-start = (bf16[4,196,2048]{2,0,1:T(4,128)(2,1)S(1)}, bf16[4,196,2048]{2,0,1:T(4,128)(2,1)}, u32[]{:S(2)}) copy-start(bf16[4,196,2048]{2,0,1:T(4,128)(2,1)} %param.14) | copy-start | bytes 9633796
  12.5 206.3 %all-to-all-start = ((bf16[64,32,2048]{2,1,0:T(8,128)(2,1)}), bf16[64,32,2048]{2,1,0:T(8,128)(2,1)}, u32[]{:S(2)}, u32[]{:S(2)}) async-start(bf16[64,32,2048]{2,1,0:T(8,128)(2,1)} %stack.39), calls=%async_computation | async-start | bytes 16777216 | tf_op jit(solution)/shard_map/all_to_all | solution.py:16
  24.6 913.2 %reduce-scatter.2.cloned.1.call-start = ((), (), s32[]{:S(2)}) async-start(), calls=%async_computation.2 | async-start | bytes 17039360 | tf_op jit(solution)/shard_map/reduce_scatter | solution.py:204
  24.7 2.6 copy-start.11
  32.2 2.3 copy-start.3
  32.2 4.1 copy-start.8
  32.2 2.2 copy-start.15
  34.5 3.5 copy-start.10
  42.7 2.4 copy-start.9
  229.4 3.1 copy-start.6
  239.2 1.9 copy-start.7
  244.7 10.5 %collective-permute-start = (bf16[98,2048]{1,0:T(8,128)(2,1)}, bf16[98,2048]{1,0:T(8,128)(2,1)S(1)}, u32[]{:S(2)}, u32[]{:S(2)}) collective-permute-start(bf16[98,2048]{1,0:T(8,128)(2,1)} %get-tuple-element.688), channel_id=1, source_target_pairs={{64,0},{128,64},{192,128},{65,1},{129,65},{193,129},{66,2},{130,66... | collective-permute-start | bytes 1204232 | tf_op jit(solution)/shard_map/while/body/eval_jaxpr/ppermute | solution.py:25
  263.7 3.1 copy-start.6
  273.5 1.9 copy-start.7
  279.0 12.6 %collective-permute-start = (bf16[98,2048]{1,0:T(8,128)(2,1)}, bf16[98,2048]{1,0:T(8,128)(2,1)S(1)}, u32[]{:S(2)}, u32[]{:S(2)}) collective-permute-start(bf16[98,2048]{1,0:T(8,128)(2,1)} %get-tuple-element.688), channel_id=1, source_target_pairs={{64,0},{128,64},{192,128},{65,1},{129,65},{193,129},{66,2},{130,66... | collective-permute-start | bytes 1204232 | tf_op jit(solution)/shard_map/while/body/eval_jaxpr/ppermute | solution.py:25
  300.2 3.1 copy-start.6
  315.5 11.7 %collective-permute-start = (bf16[98,2048]{1,0:T(8,128)(2,1)}, bf16[98,2048]{1,0:T(8,128)(2,1)S(1)}, u32[]{:S(2)}, u32[]{:S(2)}) collective-permute-start(bf16[98,2048]{1,0:T(8,128)(2,1)} %get-tuple-element.688), channel_id=1, source_target_pairs={{64,0},{128,64},{192,128},{65,1},{129,65},{193,129},{66,2},{130,66... | collective-permute-start | bytes 1204232 | tf_op jit(solution)/shard_map/while/body/eval_jaxpr/ppermute | solution.py:25
  335.8 3.1 copy-start.6
  345.6 1.9 copy-start.7
  351.1 11.0 %collective-permute-start = (bf16[98,2048]{1,0:T(8,128)(2,1)}, bf16[98,2048]{1,0:T(8,128)(2,1)S(1)}, u32[]{:S(2)}, u32[]{:S(2)}) collective-permute-start(bf16[98,2048]{1,0:T(8,128)(2,1)} %get-tuple-element.688), channel_id=1, source_target_pairs={{64,0},{128,64},{192,128},{65,1},{129,65},{193,129},{66,2},{130,66... | collective-permute-start | bytes 1204232 | tf_op jit(solution)/shard_map/while/body/eval_jaxpr/ppermute | solution.py:25
  370.7 3.1 copy-start.6
  380.5 1.9 copy-start.7
  386.0 10.8 %collective-permute-start = (bf16[98,2048]{1,0:T(8,128)(2,1)}, bf16[98,2048]{1,0:T(8,128)(2,1)S(1)}, u32[]{:S(2)}, u32[]{:S(2)}) collective-permute-start(bf16[98,2048]{1,0:T(8,128)(2,1)} %get-tuple-element.688), channel_id=1, source_target_pairs={{64,0},{128,64},{192,128},{65,1},{129,65},{193,129},{66,2},{130,66... | collective-permute-start | bytes 1204232 | tf_op jit(solution)/shard_map/while/body/eval_jaxpr/ppermute | solution.py:25
  406.6 532.9 %copy-start.1 = (bf16[4,196,2048]{2,0,1:T(4,128)(2,1)S(1)}, bf16[4,196,2048]{2,0,1:T(4,128)(2,1)}, u32[]{:S(2)}) copy-start(bf16[4,196,2048]{2,0,1:T(4,128)(2,1)} %param.14) | copy-start | bytes 9633796
  (16 other events, 23.5 us)
Sparse Core Ops, SparseCore 0:
  406.8 531.0 reduce-scatter.1
